TPU v7x, 128 devices: a whole 4x4x4 slice. The times are simulated.
128 devices in a mesh: row: 8 (over z, x_lo), col: 16 (over x_hi, y, core).
Axes of the slice: x: 4 (x_hi: 2, x_lo: 2; x = x_hi * 2 + x_lo), y: 4, z: 4, core: 2. Of those that a mesh axis runs over, the one named last changes fastest.
Arguments:
- tokens: bfloat16 [8192, 2048], P(('row', 'col')), may hold values from -6 to 6
- timestep: int32 [1], replicated, may hold values from 0 to 999
- mod_weight: float32 [256, 2048], replicated, may hold values from -0.375 to 0.375
- qkv_weight: bfloat16 [3, 2048, 2048], P(None, None, 'col'), may hold values from -0.125 to 0.125
- attn_scale: float32 [16], P('col'), may hold values from 4 to 40
- out_weight: bfloat16 [2048, 2048], P('col'), may hold values from -0.5 to 0.5
- grad_update: bfloat16 [8192, 2048], P(('row', 'col')), may hold values from -6 to 6
Outputs:
- update: bfloat16 [8192, 2048], P(('row', 'col'))
- grad_tokens: bfloat16 [8192, 2048], P(('row', 'col'))
- grad_qkv: float32 [3, 2048, 2048], P(None, 'row', 'col')
- grad_out: float32 [2048, 2048], P('col', 'row')
All inputs are finite; a program needn't handle non-finite values.
Results may differ from a plain program's by a relative error of at most 0.018.
Values may be sent and summed in bfloat16 or wider, within the bound.
No kernel may reach another device: no remote copies, remote signals or barrier semaphores. Data moves between devices by JAX's collectives and lax.ppermute only.
A program may use at most 128 MiB of HBM per device.

v0:
```python
import math
import jax
import jax.numpy as jnp
from jax import lax
from jax.sharding import PartitionSpec as P

epsilon = 1e-06


def sent_together(arrays, axis, dim, along):
    widths = [a.shape[along] for a in arrays]
    both = jnp.concatenate(arrays, axis=along)
    whole = lax.all_gather(both, axis, axis=dim, tiled=True)
    return tuple(jnp.split(whole, [sum(widths[:k]) for k in range(1, len(widths))], axis=along))


def cut_along(shard, dim, count):
    shape = shard.shape
    tiles = shard.reshape(*shape[:dim], count, shape[dim] // count, *shape[dim + 1 :])
    return jnp.moveaxis(tiles, dim, 0)


def sum_at_owner(shard, axis, dim):
    count = lax.axis_size(axis)
    tiles = lax.all_to_all(cut_along(shard, dim, count), axis, 0, 0, tiled=True)
    return jnp.sum(tiles.astype(jnp.float32), axis=0)


def embed(timestep, count):
    index = jnp.arange(count, dtype=jnp.float32)
    freqs = jnp.exp(-math.log(10000.0) * index / count)
    angles = timestep.astype(jnp.float32)[0] * freqs
    return jnp.concatenate([jnp.cos(angles), jnp.sin(angles)])


def unit_rows(values):
    factor = lax.rsqrt(jnp.mean(values * values, -1, keepdims=True) + epsilon)
    return (values * factor, factor)


def unit_grad(grad_unit, unit, factor):
    return factor * (grad_unit - unit * jnp.mean(grad_unit * unit, -1, keepdims=True))


def split_blocks(array, size):
    return array.reshape((array.shape[0] // size, size) + array.shape[1:])


def per_device(tokens, timestep, mod_weight, qkv_weight, attn_scale, out_weight, grad_update):
    tok_dev, width = tokens.shape
    heads_here = attn_scale.shape[0]
    inner = qkv_weight.shape[2]
    head_dim = inner // heads_here
    span = tok_dev * lax.axis_size("col")
    coeff = attn_scale / head_dim
    embedded = embed(timestep, mod_weight.shape[0] // 2)
    gain = 1.0 + jnp.sum(embedded[:, None] * mod_weight, 0)
    tok_float = tokens.astype(jnp.float32)
    rstd = lax.rsqrt(jnp.mean(tok_float * tok_float, -1, keepdims=True) + epsilon)
    normed = tok_float * rstd
    hidden = (normed * gain).astype(jnp.bfloat16)
    group = lax.all_gather(hidden, "col", axis=0, tiled=True)
    raw = jnp.einsum("sd,kdh->ksh", group, qkv_weight, preferred_element_type=jnp.float32)
    query_unit, query_factor = unit_rows(raw[0].reshape(span, heads_here, head_dim))
    key_unit, key_factor = unit_rows(raw[1].reshape(span, heads_here, head_dim))
    queries = query_unit.astype(jnp.bfloat16)
    key_heads = key_unit.astype(jnp.bfloat16)
    value_heads = raw[2].astype(jnp.bfloat16).reshape(span, heads_here, head_dim)
    start_state = (
        jnp.zeros((heads_here, span), jnp.float32),
        jnp.zeros((span, heads_here, head_dim), jnp.float32),
    )
    carry = start_state
    key_piece, value_piece = sent_together((key_heads, value_heads), "row", 0, 1)
    size = math.gcd(key_piece.shape[0], 512)

    def attend_step(state, block):
        key_block, value_block = block
        scores = (
            jnp.einsum("qhd,khd->hqk", queries, key_block, preferred_element_type=jnp.float32)
            * coeff[:, None, None]
        )
        weights = jnp.exp(scores - attn_scale[:, None, None])
        totals = state[0] + jnp.sum(weights, -1)
        mixed = state[1] + jnp.einsum(
            "hqk,khd->qhd",
            weights.astype(jnp.bfloat16),
            value_block,
            preferred_element_type=jnp.float32,
        )
        return ((totals, mixed), None)

    carry, unused = lax.scan(
        attend_step, carry, (split_blocks(key_piece, size), split_blocks(value_piece, size))
    )
    totals, mixed = carry
    attended_heads = (mixed / totals.T[:, :, None]).astype(jnp.bfloat16)
    attended = attended_heads.reshape(span, inner)
    own_rows = lax.all_to_all(attended, "col", split_axis=0, concat_axis=1, tiled=True)
    update = jnp.dot(
        own_rows,
        lax.all_gather(out_weight, "col", axis=0, tiled=True),
        preferred_element_type=jnp.float32,
    ).astype(jnp.bfloat16)
    grad_group = lax.all_gather(grad_update, "col", axis=0, tiled=True)
    out_part = lax.dot_general(
        attended, grad_group, (((0,), (0,)), ((), ())), preferred_element_type=jnp.float32
    )
    grad_out = sum_at_owner(out_part.astype(jnp.bfloat16), "row", 1)
    grad_attended = lax.dot_general(
        grad_group, out_weight, (((1,), (1,)), ((), ())), preferred_element_type=jnp.float32
    ).astype(jnp.bfloat16)
    grad_heads = grad_attended.reshape(span, heads_here, head_dim)
    delta = jnp.sum(grad_heads.astype(jnp.float32) * attended_heads.astype(jnp.float32), -1)
    inverse = 1.0 / totals

    def pair_terms(query_rows, grad_rows, inverse_rows, delta_rows, key_block, value_block):
        scores = (
            jnp.einsum("qhd,khd->hqk", query_rows, key_block, preferred_element_type=jnp.float32)
            * coeff[:, None, None]
        )
        probs = jnp.exp(scores - attn_scale[:, None, None]) * inverse_rows[:, :, None]
        dprobs = jnp.einsum(
            "qhd,khd->hqk", grad_rows, value_block, preferred_element_type=jnp.float32
        )
        dscores = (probs * (dprobs - delta_rows[:, :, None]) * coeff[:, None, None]).astype(
            jnp.bfloat16
        )
        return (probs, dscores)

    empty_own = jnp.zeros((span, heads_here, head_dim), jnp.float32)
    carry = empty_own
    key_piece, value_piece = sent_together((key_heads, value_heads), "row", 0, 1)
    size = math.gcd(key_piece.shape[0], 512)

    def query_step(state, block):
        key_block, value_block = block
        probs, dscores = pair_terms(queries, grad_heads, inverse, delta.T, key_block, value_block)
        return (
            state
            + jnp.einsum("hqk,khd->qhd", dscores, key_block, preferred_element_type=jnp.float32),
            None,
        )

    carry, unused = lax.scan(
        query_step, carry, (split_blocks(key_piece, size), split_blocks(value_piece, size))
    )
    grad_query = carry
    all_inverse, all_delta = sent_together((inverse.T, delta), "row", 0, 1)
    carry = (empty_own, empty_own)
    query_piece, grad_piece = sent_together((queries, grad_heads), "row", 0, 1)
    count = query_piece.shape[0]
    size = math.gcd(count, 512)

    def key_step(state, block):
        query_block, grad_block, inverse_block, delta_block = block
        probs, dscores = pair_terms(
            query_block, grad_block, inverse_block.T, delta_block.T, key_heads, value_heads
        )
        grad_key = state[0] + jnp.einsum(
            "hqk,qhd->khd", dscores, query_block, preferred_element_type=jnp.float32
        )
        grad_value = state[1] + jnp.einsum(
            "hqk,qhd->khd",
            probs.astype(jnp.bfloat16),
            grad_block,
            preferred_element_type=jnp.float32,
        )
        return ((grad_key, grad_value), None)

    carry, unused = lax.scan(
        key_step,
        carry,
        (
            split_blocks(query_piece, size),
            split_blocks(grad_piece, size),
            split_blocks(all_inverse, size),
            split_blocks(all_delta, size),
        ),
    )
    grad_key, grad_value = carry
    grad_q = (
        unit_grad(grad_query, query_unit, query_factor).astype(jnp.bfloat16).reshape(span, inner)
    )
    grad_k = unit_grad(grad_key, key_unit, key_factor).astype(jnp.bfloat16).reshape(span, inner)
    grad_v = grad_value.astype(jnp.bfloat16).reshape(span, inner)
    grad_raw = jnp.stack([grad_q, grad_k, grad_v])
    qkv_part = jnp.einsum("sd,ksh->kdh", group, grad_raw, preferred_element_type=jnp.float32)
    grad_qkv = sum_at_owner(qkv_part.astype(jnp.bfloat16), "row", 1)
    grad_hidden = lax.psum_scatter(
        jnp.einsum("ksh,kdh->sd", grad_raw, qkv_weight, preferred_element_type=jnp.float32).astype(
            jnp.bfloat16
        ),
        "col",
        scatter_dimension=0,
        tiled=True,
    ).astype(jnp.float32)
    grad_normed = grad_hidden * gain
    grad_tokens = (
        rstd * (grad_normed - normed * jnp.mean(grad_normed * normed, -1, keepdims=True))
    ).astype(jnp.bfloat16)
    return (update, grad_tokens, grad_qkv, grad_out)


def solution(mesh):
    placed = (
        P(("row", "col"), None),
        P(),
        P(),
        P(None, None, "col"),
        P("col"),
        P("col", None),
        P(("row", "col"), None),
    )
    return jax.shard_map(
        per_device,
        mesh=mesh,
        in_specs=placed,
        out_specs=(
            P(("row", "col"), None),
            P(("row", "col"), None),
            P(None, "row", "col"),
            P("col", "row"),
        ),
        check_vma=False,
    )
```

profile of v0, /device:TPU:0, one launch (start us, length us, event | category | flops | bytes accessed | tf_op | source)
XLA Modules:
  0.0 560.1 jit_solution(7226077583093130001)
XLA Ops:
  11.7 56.6 %all-gather.6.cloned.1.call-done = bf16[1024,2048]{1,0:T(8,128)(2,1)} async-done(((bf16[64,2048]{1,0:T(8,128)(2,1)}), bf16[1024,2048]{1,0:T(8,128)(2,1)}) %all-gather.6.cloned.1.call-update) | async-done | bytes 4194320 | tf_op jit(solution)/shard_map/all_gather | solution.py:62
  68.3 4.0 fusion.93
  76.1 87.4 %all-gather.8.cloned.1.call-done = bf16[8192,2,128]{0,2,1:T(8,128)(2,1)} async-done(((bf16[1024,2,128]{0,2,1:T(8,128)(2,1)}), bf16[8192,2,128]{0,2,1:T(8,128)(2,1)}) %all-gather.8.cloned.1.call-update) | async-done | bytes 4194320 | tf_op jit(solution)/shard_map/all_gather | solution.py:13
  163.5 3.9 fusion.91
  167.4 4.1 copy.61
  171.5 2.5 copy.62
  174.0 68.0 %while.37 = (s32[]{:T(128)}, f32[1,1024]{1,0:T(1,128)S(1)}, f32[1024,1,128]{0,2,1:T(8,128)S(1)}, bf16[16,512,1,128]{3,1,2,0:T(8,128)(2,1)}, bf16[1024,1,128]{2,0...) while((s32[]{:T(128)}, f32[1,1024]{1,0:T(1,128)S(1)}, ...), condition=%wide.region_6.7_spmd.clone, body=%wide.region_4.6_spmd.clone.sunk | while | flops 271844352 | bytes 5786736 | solution.py:93
  176.1 2.1 fusion.128
  188.8 2.1 fusion.128
  193.1 2.1 fusion.128
  197.3 2.1 fusion.128
  201.6 2.1 fusion.128
  205.8 2.1 fusion.128
  218.6 2.1 fusion.128
  242.0 4.5 multiply_reduce_fusion.3
  250.6 79.5 %while.38 = (s32[]{:T(128)}, f32[1024,1,128]{0,2,1:T(8,128)}, bf16[16,512,1,128]{3,1,2,0:T(8,128)(2,1)}, bf16[1024,1,128]{2,0,1:T(8,128)(2,1)S(1)}, f32[1]{0:T(1...) while((s32[]{:T(128)}, f32[1024,1,128]{0,2,1:T(8,128)}, ...), condition=%wide.region_9.10_spmd.clone, body=%wide.region_8.9_spmd.clone.sunk | while | flops 406585344 | bytes 6171263 | solution.py:145
  251.9 3.5 fusion.135
  256.7 3.6 fusion.135
  261.7 3.7 fusion.135
  266.7 3.6 fusion.135
  271.7 3.6 fusion.135
  276.6 3.6 fusion.135
  281.6 3.6 fusion.135
  286.6 3.6 fusion.135
  291.6 3.6 fusion.135
  296.5 3.6 fusion.135
  301.5 3.6 fusion.135
  306.5 3.7 fusion.135
  311.5 3.6 fusion.135
  316.5 3.6 fusion.135
  321.4 3.6 fusion.135
  326.4 3.6 fusion.135
  330.1 28.7 %all_gather.24 = f32[8192,2]{0,1:T(2,128)S(1)} all-gather(f32[1024,2]{0,1:T(2,128)S(1)} %pad_maximum_fusion.5), channel_id=1, replica_groups=mesh['row'=8,'col'=16] {'row'}, dimensions={0}, use_global_device_ids=true | all-gather | bytes 73728 | tf_op jit(solution)/shard_map/all_gather | solution.py:13
  358.9 3.9 fusion.90
  362.8 4.1 copy.59
  366.9 2.4 copy.60
  369.3 82.8 %while.39 = (s32[]{:T(128)}, f32[1024,1,128]{0,2,1:T(8,128)S(1)}, f32[1024,1,128]{0,2,1:T(8,128)S(1)}, bf16[16,512,1,128]{3,1,2,0:T(8,128)(2,1)}, bf16[1024,1,12...) while((s32[]{:T(128)}, f32[1024,1,128]{0,2,1:T(8,128)S(1)}, ...), condition=%wide.region_12.13_spmd.clone, body=%wide.region_11.12_spmd.clone.sunk | while | flops 541589504 | bytes 9453196 | solution.py:171
  455.3 4.3 bitcast_convert_fusion
  461.4 6.6 %all-to-all-start = ((bf16[16,64,128]{2,1,0:T(8,128)(2,1)}), bf16[16,64,128]{2,1,0:T(8,128)(2,1)S(1)}, u32[]{:S(2)}, u32[]{:S(2)}) async-start(bf16[16,64,128]{2,1,0:T(8,128)(2,1)} %bitcast.10), calls=%async_computation | async-start | bytes 524288 | tf_op jit(solution)/shard_map/all_to_all | solution.py:99
  468.0 3.1 convolution_convert_fusion
  472.0 5.5 all-to-all-done
  477.5 3.5 all-to-all-start.2
  481.0 4.1 fusion.63
  486.4 4.6 all-to-all-done.2
  491.1 3.6 all-to-all-start.1
  495.4 5.7 %convolution_convert_fusion.1 = bf16[64,2048]{1,0:T(8,128)(2,1)} fusion(bf16[2048,2048]{1,0:T(8,128)(2,1)} %all-gather.10.cloned.1.call-done, bf16[16,64,128]{2,1,0:T(8,128)(2,1)S(1)} %all-to-all-done), kind=kOutput, calls=%fused_computation.67 | convolution fusion | flops 537001984 | bytes 8912896 | tf_op jit(solution)/shard_map/dot_general | solution.py:100
  501.1 24.3 %all-to-all-done.1 = bf16[8,3,256,128]{2,3,1,0:T(8,128)(2,1)S(1)} async-done(((bf16[8,3,256,128]{2,3,1,0:T(8,128)(2,1)}), bf16[8,3,256,128]{2,3,1,0:T(8,128)(2,1)S(1)}, u32[]{:S(2)}, u32[]{:S(2)}) %all-to-all-start.1) | async-done | bytes 1572896 | tf_op jit(solution)/shard_map/all_to_all | solution.py:25
  526.5 23.7 %reduce-scatter.2.cloned.1.call-done = bf16[64,2048]{1,0:T(8,128)(2,1)} async-done(((bf16[1024,2048]{1,0:T(8,128)(2,1)}), bf16[64,2048]{1,0:T(8,128)(2,1)}) %reduce-scatter.2.cloned.1.call-update) | async-done | bytes 262160 | tf_op jit(solution)/shard_map/reduce_scatter | solution.py:190
  (200 shorter events, 178.8 us)
Async XLA Ops:
  7.2 2.7 copy-start.3
  7.2 3.8 copy-start.8
  7.2 61.1 %all-gather.6.cloned.1.call-start = ((), (), s32[]{:S(2)}) async-start(), calls=%async_computation.4 | async-start | bytes 4456448 | tf_op jit(solution)/shard_map/all_gather | solution.py:62
  10.9 152.6 %all-gather.8.cloned.1.call-start = ((), (), s32[]{:S(2)}) async-start(), calls=%async_computation.5 | async-start | bytes 4718592 | tf_op jit(solution)/shard_map/all_gather | solution.py:13
  72.3 1.2 copy-start
  73.6 2.5 copy-start.5
  74.5 167.5 %all-gather.12.cloned.1.call-start = ((), (), s32[]{:S(2)}) async-start(), calls=%async_computation.7 | async-start | bytes 4456448 | tf_op jit(solution)/shard_map/all_gather | solution.py:105
  75.2 283.6 %all-gather.14.cloned.1.call-start = ((), (), s32[]{:S(2)}) async-start(), calls=%async_computation.8 | async-start | bytes 4718592 | tf_op jit(solution)/shard_map/all_gather | solution.py:13
  242.0 4.5 copy-start.6
  247.3 248.1 %all-gather.10.cloned.1.call-start = ((), (), s32[]{:S(2)}) async-start(), calls=%async_computation.6 | async-start | bytes 8912896 | tf_op jit(solution)/shard_map/all_gather | solution.py:102
  247.9 302.3 %reduce-scatter.2.cloned.1.call-start = ((), (), s32[]{:S(2)}) async-start(), calls=%async_computation.9 | async-start | bytes 4456448 | tf_op jit(solution)/shard_map/reduce_scatter | solution.py:190
  366.9 2.4 copy-start.2
  452.1 1.9 copy-start.1
  452.1 2.0 copy-start.7
  453.8 1.5 copy-start.9
  459.6 0.9 copy-start.10
  461.4 16.1 %all-to-all-start = ((bf16[16,64,128]{2,1,0:T(8,128)(2,1)}), bf16[16,64,128]{2,1,0:T(8,128)(2,1)S(1)}, u32[]{:S(2)}, u32[]{:S(2)}) async-start(bf16[16,64,128]{2,1,0:T(8,128)(2,1)} %bitcast.10), calls=%async_computation | async-start | bytes 524288 | tf_op jit(solution)/shard_map/all_to_all | solution.py:99
  477.5 13.6 %all-to-all-start.2 = ((bf16[8,128,256]{2,1,0:T(8,128)(2,1)}), bf16[8,128,256]{2,1,0:T(8,128)(2,1)S(1)}, u32[]{:S(2)}, u32[]{:S(2)}) async-start(bf16[8,128,256]{2,1,0:T(8,128)(2,1)} %bitcast.177), calls=%async_computation.3 | async-start | bytes 1048576 | tf_op jit(solution)/shard_map/all_to_all | solution.py:25
  491.1 34.3 %all-to-all-start.1 = ((bf16[8,3,256,128]{2,3,1,0:T(8,128)(2,1)}), bf16[8,3,256,128]{2,3,1,0:T(8,128)(2,1)S(1)}, u32[]{:S(2)}, u32[]{:S(2)}) async-start(bf16[8,3,256,128]{2,3,1,0:T(8,128)(2,1)} %bitcast.175), calls=%async_computation.2 | async-start | bytes 3145728 | tf_op jit(solution)/shard_map/all_to_all | solution.py:25
  501.1 49.1 %copy-start.4 = (bf16[64,2048]{1,0:T(8,128)(2,1)S(1)}, bf16[64,2048]{1,0:T(8,128)(2,1)}, u32[]{:S(2)}) copy-start(bf16[64,2048]{1,0:T(8,128)(2,1)} %param.13) | copy-start | bytes 786436
Sparse Core Ops, SparseCore 0:
  11.1 57.1 all-gather.5
  74.6 88.8 all-gather.7
  166.0 54.3 all-gather.11
  247.5 90.8 all-gather.13
  340.7 72.3 all-gather.9
  459.8 90.3 reduce-scatter.1
where the time goes:
time: 564 us; the launch traced here: 560 us
  matrix products  254 us (45%)
  waiting for transfers between devices  203 us (36%)
  local copies, waits for them, and re-layouts  31.6 us (6%)
  blocking collectives  28.7 us (5%)
  between operations  15.9 us (3%)
  starting transfers between devices  13.9 us (2%)
  other arithmetic  11 us (2%)
    all_gather x2, waiting for transfers between devices, sent_together(): whole = lax.all_gather(both, axis, axis=dim, tiled=True)  87.4 us
    dot_general x16, matrix products, query_step(): jnp.einsum('hqk,khd->qhd', dscores, key_block, preferred_element_type=jnp...  57.9 us
    all_gather x1, waiting for transfers between devices, per_device(): group = lax.all_gather(hidden, 'col', axis=0, tiled=True)  56.6 us
    dot_general x32, matrix products, pair_terms(): jnp.einsum('qhd,khd->hqk', query_rows, key_block, preferred_element_type=...  54.5 us
    dot_general x16, matrix products, attend_step(): jnp.einsum('hqk,khd->qhd', weights.astype(jnp.bfloat16), value_block, pre...  33.9 us
    dot_general x16, matrix products, attend_step(): jnp.einsum('qhd,khd->hqk', queries, key_block, preferred_element_type=jnp...  33.2 us
    all_to_all x2, waiting for transfers between devices, sum_at_owner(): tiles = lax.all_to_all(cut_along(shard, dim, count), axis, 0, 0, tiled=True)  28.9 us
    all_gather x1, blocking collectives, sent_together(): whole = lax.all_gather(both, axis, axis=dim, tiled=True)  28.7 us
  transfers between devices with their start and end apart: 9, of which 6 were waited for; matrix products, arithmetic and copies ran while one was open for 49% of the time, Pallas kernels for 0%

commit v1 on v0

--- a/solution.py
+++ b/solution.py
@@ -59,7 +59,8 @@
     rstd = lax.rsqrt(jnp.mean(tok_float * tok_float, -1, keepdims=True) + epsilon)
     normed = tok_float * rstd
     hidden = (normed * gain).astype(jnp.bfloat16)
-    group = lax.all_gather(hidden, "col", axis=0, tiled=True)
+    sent = jnp.stack([hidden] * lax.axis_size("col"))
+    group = jnp.concatenate(lax.all_to_all(sent, "col", 0, 0), axis=0)
     raw = jnp.einsum("sd,kdh->ksh", group, qkv_weight, preferred_element_type=jnp.float32)
     query_unit, query_factor = unit_rows(raw[0].reshape(span, heads_here, head_dim))
     key_unit, key_factor = unit_rows(raw[1].reshape(span, heads_here, head_dim))

time: 564 us -> 581 us (1.030)
  waiting for transfers between devices: 203 us -> 212 us
  starting transfers between devices: 13.9 us -> 21.3 us
    all_gather x1 -> x0, waiting for transfers between devices: 56.6 us -> none  [per_device(): group = lax.all_gather(hidden, 'col', axis=0, tiled=True)]
    all_to_all x0 -> x1, waiting for transfers between devices: none -> 55.1 us  [per_device(): group = jnp.concatenate(lax.all_to_all(sent, 'col', 0, 0), axis=0)]
    all_gather x2, waiting for transfers between devices: 87.4 us -> 97.4 us  [sent_together(): whole = lax.all_gather(both, axis, axis=dim, tiled=True)]
    all_to_all x0 -> x1, starting transfers between devices: none -> 7.33 us  [per_device(): group = jnp.concatenate(lax.all_to_all(sent, 'col', 0, 0), axis=0)]
  transfers between devices with their start and end apart: 9 -> 9, of which waited for: 6 -> 6; matrix products, arithmetic and copies ran while one was open for 49% -> 48% of each run, Pallas kernels for 0% -> 0%
where the time goes in v1:
time: 581 us; the launch traced here: 577 us
  matrix products  254 us (44%)
  waiting for transfers between devices  212 us (36%)
  local copies, waits for them, and re-layouts  34.1 us (6%)
  blocking collectives  28.7 us (5%)
  starting transfers between devices  21.3 us (4%)
  between operations  15.5 us (3%)
  other arithmetic  10.3 us (2%)
    all_gather x2, waiting for transfers between devices, sent_together(): whole = lax.all_gather(both, axis, axis=dim, tiled=True)  97.4 us
    dot_general x16, matrix products, query_step(): jnp.einsum('hqk,khd->qhd', dscores, key_block, preferred_element_type=jnp...  58 us
    all_to_all x1, waiting for transfers between devices, per_device(): group = jnp.concatenate(lax.all_to_all(sent, 'col', 0, 0), axis=0)  55.1 us
    dot_general x32, matrix products, pair_terms(): jnp.einsum('qhd,khd->hqk', query_rows, key_block, preferred_element_type=...  54.5 us
    dot_general x16, matrix products, attend_step(): jnp.einsum('hqk,khd->qhd', weights.astype(jnp.bfloat16), value_block, pre...  33.9 us
    dot_general x16, matrix products, attend_step(): jnp.einsum('qhd,khd->hqk', queries, key_block, preferred_element_type=jnp...  33.2 us
    all_to_all x2, waiting for transfers between devices, sum_at_owner(): tiles = lax.all_to_all(cut_along(shard, dim, count), axis, 0, 0, tiled=True)  28.9 us
    all_gather x1, blocking collectives, sent_together(): whole = lax.all_gather(both, axis, axis=dim, tiled=True)  28.7 us
  transfers between devices with their start and end apart: 9, of which 6 were waited for; matrix products, arithmetic and copies ran while one was open for 48% of the time, Pallas kernels for 0%

profile of v1, /device:TPU:0, one launch (start us, length us, event | category | flops | bytes accessed | tf_op | source)
XLA Modules:
  0.0 577.3 jit_solution(15221502240902268478)
XLA Ops:
  10.1 2.5 stack.4
  12.6 7.3 %all-to-all-start = ((bf16[16,64,2048]{2,1,0:T(8,128)(2,1)}), bf16[16,64,2048]{2,1,0:T(8,128)(2,1)}, u32[]{:S(2)}, u32[]{:S(2)}) async-start(bf16[16,64,2048]{2,1,0:T(8,128)(2,1)} %stack.4), calls=%async_computation | async-start | bytes 8388608 | tf_op jit(solution)/shard_map/all_to_all | solution.py:63
  20.7 55.1 %all-to-all-done = bf16[16,64,2048]{2,1,0:T(8,128)(2,1)} async-done(((bf16[16,64,2048]{2,1,0:T(8,128)(2,1)}), bf16[16,64,2048]{2,1,0:T(8,128)(2,1)}, u32[]{:S(2)}, u32[]{:S(2)}) %all-to-all-start) | async-done | bytes 4194336 | tf_op jit(solution)/shard_map/all_to_all | solution.py:63
  75.8 4.0 fusion.88
  83.6 97.3 %all-gather.5.cloned.1.call-done = bf16[8192,2,128]{0,2,1:T(8,128)(2,1)} async-done(((bf16[1024,2,128]{0,2,1:T(8,128)(2,1)}), bf16[8192,2,128]{0,2,1:T(8,128)(2,1)}) %all-gather.5.cloned.1.call-update) | async-done | bytes 4194320 | tf_op jit(solution)/shard_map/all_gather | solution.py:13
  181.0 3.9 fusion.86
  184.9 4.1 copy.61
  188.9 2.5 copy.62
  191.4 68.0 %while.37 = (s32[]{:T(128)}, f32[1,1024]{1,0:T(1,128)S(1)}, f32[1024,1,128]{0,2,1:T(8,128)S(1)}, bf16[16,512,1,128]{3,1,2,0:T(8,128)(2,1)}, bf16[1024,1,128]{2,0...) while((s32[]{:T(128)}, f32[1,1024]{1,0:T(1,128)S(1)}, ...), condition=%wide.region_6.7_spmd.clone, body=%wide.region_4.6_spmd.clone.sunk | while | flops 271844352 | bytes 5786736 | solution.py:94
  193.5 2.1 fusion.124
  206.3 2.1 fusion.124
  214.8 2.1 fusion.124
  219.0 2.1 fusion.124
  236.0 2.1 fusion.124
  259.4 4.5 multiply_reduce_fusion.3
  268.0 79.5 %while.38 = (s32[]{:T(128)}, f32[1024,1,128]{0,2,1:T(8,128)}, bf16[16,512,1,128]{3,1,2,0:T(8,128)(2,1)}, bf16[1024,1,128]{2,0,1:T(8,128)(2,1)S(1)}, f32[1]{0:T(1...) while((s32[]{:T(128)}, f32[1024,1,128]{0,2,1:T(8,128)}, ...), condition=%wide.region_9.10_spmd.clone, body=%wide.region_8.9_spmd.clone.sunk | while | flops 406585344 | bytes 6171263 | solution.py:146
  269.4 3.5 fusion.131
  274.2 3.6 fusion.131
  279.2 3.7 fusion.131
  284.2 3.6 fusion.131
  289.1 3.6 fusion.131
  294.1 3.6 fusion.131
  299.1 3.6 fusion.131
  304.1 3.6 fusion.131
  309.1 3.6 fusion.131
  314.0 3.6 fusion.131
  319.0 3.6 fusion.131
  324.0 3.7 fusion.131
  329.0 3.6 fusion.131
  333.9 3.6 fusion.131
  338.9 3.6 fusion.131
  343.9 3.6 fusion.131
  347.5 28.7 %all_gather.20 = f32[8192,2]{0,1:T(2,128)S(1)} all-gather(f32[1024,2]{0,1:T(2,128)S(1)} %pad_maximum_fusion.5), channel_id=1, replica_groups=mesh['row'=8,'col'=16] {'row'}, dimensions={0}, use_global_device_ids=true | all-gather | bytes 73728 | tf_op jit(solution)/shard_map/all_gather | solution.py:13
  376.3 3.9 fusion.85
  380.3 4.1 copy.59
  384.3 2.4 copy.60
  386.8 82.8 %while.39 = (s32[]{:T(128)}, f32[1024,1,128]{0,2,1:T(8,128)S(1)}, f32[1024,1,128]{0,2,1:T(8,128)S(1)}, bf16[16,512,1,128]{3,1,2,0:T(8,128)(2,1)}, bf16[1024,1,12...) while((s32[]{:T(128)}, f32[1024,1,128]{0,2,1:T(8,128)S(1)}, ...), condition=%wide.region_12.13_spmd.clone, body=%wide.region_11.12_spmd.clone.sunk | while | flops 541589504 | bytes 9453196 | solution.py:172
  472.8 4.3 bitcast_convert_fusion
  478.9 6.6 %all-to-all-start.1 = ((bf16[16,64,128]{2,1,0:T(8,128)(2,1)}), bf16[16,64,128]{2,1,0:T(8,128)(2,1)S(1)}, u32[]{:S(2)}, u32[]{:S(2)}) async-start(bf16[16,64,128]{2,1,0:T(8,128)(2,1)} %bitcast.11), calls=%async_computation.1 | async-start | bytes 524288 | tf_op jit(solution)/shard_map/all_to_all | solution.py:100
  485.5 3.1 convolution_convert_fusion.1
  489.5 5.5 all-to-all-done.1
  495.0 3.5 all-to-all-start.3
  498.5 4.1 convolution_convert_fusion
  503.9 4.6 all-to-all-done.3
  508.6 3.6 all-to-all-start.2
  512.9 5.7 convolution_convert_fusion.2
  518.6 24.3 %all-to-all-done.2 = bf16[8,3,256,128]{2,3,1,0:T(8,128)(2,1)S(1)} async-done(((bf16[8,3,256,128]{2,3,1,0:T(8,128)(2,1)}), bf16[8,3,256,128]{2,3,1,0:T(8,128)(2,1)S(1)}, u32[]{:S(2)}, u32[]{:S(2)}) %all-to-all-start.2) | async-done | bytes 1572896 | tf_op jit(solution)/shard_map/all_to_all | solution.py:25
  544.0 23.8 %reduce-scatter.2.cloned.1.call-done = bf16[64,2048]{1,0:T(8,128)(2,1)} async-done(((bf16[1024,2048]{1,0:T(8,128)(2,1)}), bf16[64,2048]{1,0:T(8,128)(2,1)}) %reduce-scatter.2.cloned.1.call-update) | async-done | bytes 262160 | tf_op jit(solution)/shard_map/reduce_scatter | solution.py:191
  (200 shorter events, 182.3 us)
Async XLA Ops:
  7.2 2.6 copy-start.3
  12.6 7.4 %copy-start.8 = (bf16[3,2048,128]{2,1,0:T(8,128)(2,1)S(1)}, bf16[3,2048,128]{2,1,0:T(8,128)(2,1)}, u32[]{:S(2)}) copy-start(bf16[3,2048,128]{2,1,0:T(8,128)(2,1)} %param.16) | copy-start | bytes 4718596
  12.6 63.2 %all-to-all-start = ((bf16[16,64,2048]{2,1,0:T(8,128)(2,1)}), bf16[16,64,2048]{2,1,0:T(8,128)(2,1)}, u32[]{:S(2)}, u32[]{:S(2)}) async-start(bf16[16,64,2048]{2,1,0:T(8,128)(2,1)} %stack.4), calls=%async_computation | async-start | bytes 8388608 | tf_op jit(solution)/shard_map/all_to_all | solution.py:63
  19.9 161.1 %all-gather.5.cloned.1.call-start = ((), (), s32[]{:S(2)}) async-start(), calls=%async_computation.5 | async-start | bytes 4718592 | tf_op jit(solution)/shard_map/all_gather | solution.py:13
  79.8 1.2 copy-start
  81.1 2.6 copy-start.5
  82.0 177.5 %all-gather.9.cloned.1.call-start = ((), (), s32[]{:S(2)}) async-start(), calls=%async_computation.7 | async-start | bytes 4456448 | tf_op jit(solution)/shard_map/all_gather | solution.py:106
  82.7 293.6 %all-gather.11.cloned.1.call-start = ((), (), s32[]{:S(2)}) async-start(), calls=%async_computation.8 | async-start | bytes 4718592 | tf_op jit(solution)/shard_map/all_gather | solution.py:13
  259.4 4.5 copy-start.6
  264.8 248.1 %all-gather.7.cloned.1.call-start = ((), (), s32[]{:S(2)}) async-start(), calls=%async_computation.6 | async-start | bytes 8912896 | tf_op jit(solution)/shard_map/all_gather | solution.py:103
  265.4 302.3 %reduce-scatter.2.cloned.1.call-start = ((), (), s32[]{:S(2)}) async-start(), calls=%async_computation.9 | async-start | bytes 4456448 | tf_op jit(solution)/shard_map/reduce_scatter | solution.py:191
  384.3 2.4 copy-start.2
  469.5 1.9 copy-start.1
  469.6 2.0 copy-start.7
  471.3 1.5 copy-start.9
  477.1 0.9 copy-start.10
  478.9 16.1 %all-to-all-start.1 = ((bf16[16,64,128]{2,1,0:T(8,128)(2,1)}), bf16[16,64,128]{2,1,0:T(8,128)(2,1)S(1)}, u32[]{:S(2)}, u32[]{:S(2)}) async-start(bf16[16,64,128]{2,1,0:T(8,128)(2,1)} %bitcast.11), calls=%async_computation.1 | async-start | bytes 524288 | tf_op jit(solution)/shard_map/all_to_all | solution.py:100
  495.0 13.6 %all-to-all-start.3 = ((bf16[8,128,256]{2,1,0:T(8,128)(2,1)}), bf16[8,128,256]{2,1,0:T(8,128)(2,1)S(1)}, u32[]{:S(2)}, u32[]{:S(2)}) async-start(bf16[8,128,256]{2,1,0:T(8,128)(2,1)} %bitcast.176), calls=%async_computation.4 | async-start | bytes 1048576 | tf_op jit(solution)/shard_map/all_to_all | solution.py:25
  508.6 34.3 %all-to-all-start.2 = ((bf16[8,3,256,128]{2,3,1,0:T(8,128)(2,1)}), bf16[8,3,256,128]{2,3,1,0:T(8,128)(2,1)S(1)}, u32[]{:S(2)}, u32[]{:S(2)}) async-start(bf16[8,3,256,128]{2,3,1,0:T(8,128)(2,1)} %bitcast.174), calls=%async_computation.3 | async-start | bytes 3145728 | tf_op jit(solution)/shard_map/all_to_all | solution.py:25
  518.6 49.1 %copy-start.4 = (bf16[64,2048]{1,0:T(8,128)(2,1)S(1)}, bf16[64,2048]{1,0:T(8,128)(2,1)}, u32[]{:S(2)}) copy-start(bf16[64,2048]{1,0:T(8,128)(2,1)} %param.13) | copy-start | bytes 786436
Sparse Core Ops, SparseCore 0:
  82.1 98.8 all-gather.4
  183.4 54.3 all-gather.8
  264.9 90.8 all-gather.10
  358.2 72.3 all-gather.6
  477.2 90.4 reduce-scatter.1
